TPU v7x, 32 devices: a whole 2x2x4 slice. The times are simulated.
32 devices in a mesh: dp: 8 (over y, x, core), mp: 4 (over z).
Axes of the slice: x: 2, y: 2, z: 4, core: 2. Of those that a mesh axis runs over, the one named last changes fastest.
Arguments:
- target_states: bfloat16 [1024, 4096], P('dp', 'mp')
- target_gain: float32 [4096], replicated, may hold values from 0.1 to 1.9
- target_head: bfloat16 [4096, 128256], P(None, ('dp', 'mp'))
- reference_states: bfloat16 [1024, 2048], P(('dp', 'mp'))
- reference_gain: float32 [2048], replicated, may hold values from 0.1 to 1.9
- reference_head: bfloat16 [2048, 128256], P(None, ('dp', 'mp'))
- token_ids: int32 [1024], P('dp'), may hold values from 0 to 128255
- reference_order: int32 [8], replicated, may hold values from 0 to 7, each once
Outputs:
- target_loss: float32 [1024], P('dp')
- reference_loss: float32 [1024], P('dp')
- reducible: float32 [8], P('dp')
Inputs may be any that keep to these rules, and one draw needn't show every extreme that they name: reference_states rows s * 128 to s * 128 + 127 belong to candidate sequence reference_order[s].
All inputs are finite; a program needn't handle non-finite values.
Results may differ from a plain program's by a relative error of at most 0.0041.
Values may be sent and summed in bfloat16 or wider, within the bound.
A program may use at most 128 MiB of HBM per device.

v0:
```python
import math
import jax
import jax.numpy as jnp
from jax import lax
from jax.sharding import PartitionSpec as P

LENGTH = 128
EPSILON = 1e-05


def normalize(states, gain):
    values = states.astype(jnp.float32)
    factor = lax.rsqrt(jnp.mean(values * values, axis=1, keepdims=True) + EPSILON)
    return (values * factor * gain[None, :]).astype(jnp.bfloat16)


def block_stats(logits, rows_id, columns):
    peak_val = jnp.max(logits, axis=1)
    exp_total = jnp.sum(jnp.exp(logits - peak_val[:, None]), axis=1)
    chosen = jnp.sum(jnp.where(columns[None, :] == rows_id[:, None], logits, 0.0), axis=1)
    return (peak_val, exp_total, chosen)


def shards(
    target_states,
    target_gain,
    target_head,
    reference_states,
    reference_gain,
    reference_head,
    token_ids,
    reference_order,
):
    vocab_width = target_head.shape[1]
    columns = lax.axis_index(("dp", "mp")) * vocab_width + jnp.arange(vocab_width, dtype=jnp.int32)
    rows_dp = target_states.shape[0]
    data_ways = lax.axis_size("dp")
    tokens = rows_dp * data_ways
    empty_float = jnp.zeros((tokens,), jnp.float32)
    empty_ids = jnp.zeros((tokens,), jnp.int32)
    gathered = lax.all_gather(target_states, "mp", axis=1, tiled=True)
    normed = normalize(gathered, target_gain)
    carry = (empty_float, empty_float, empty_float, empty_ids)
    start = jnp.int32(0)
    rows_x = lax.all_gather(normed, "dp", axis=0, tiled=True)
    rows_id = lax.all_gather(token_ids, "dp", axis=0, tiled=True)
    logits = jnp.dot(rows_x, target_head, preferred_element_type=jnp.float32)
    found = block_stats(logits, rows_id, columns) + (rows_id,)
    t_peak, t_total, t_pick, ids_all = tuple(
        (
            lax.dynamic_update_slice_in_dim(earlier, fresh_val, start, 0)
            for earlier, fresh_val in zip(carry, found)
        )
    )
    ref_normed = normalize(reference_states, reference_gain)
    ref_rows = lax.all_gather(ref_normed, ("dp", "mp"), axis=0, tiled=True)
    seq_count = tokens // LENGTH
    ref_ids = jnp.take(ids_all.reshape(seq_count, LENGTH), reference_order, axis=0).reshape(tokens)
    blocking = math.gcd(tokens, 512)

    def ref_block(packed):
        rows_x, rows_id = packed
        logits = jnp.dot(rows_x, reference_head, preferred_element_type=jnp.float32)
        return block_stats(logits, rows_id, columns)

    r_peak, r_total, r_pick = lax.map(
        ref_block,
        (ref_rows.reshape(-1, blocking, ref_rows.shape[1]), ref_ids.reshape(-1, blocking)),
    )
    r_peak = r_peak.reshape(tokens)
    r_total = r_total.reshape(tokens)
    r_pick = r_pick.reshape(tokens)
    t_max, r_max = lax.pmax((t_peak, r_peak), ("dp", "mp"))
    t_sum, t_hit, r_sum, r_hit = lax.psum(
        (t_total * jnp.exp(t_peak - t_max), t_pick, r_total * jnp.exp(r_peak - r_max), r_pick),
        ("dp", "mp"),
    )
    loss_target = t_max + jnp.log(t_sum) - t_hit
    loss_rows = r_max + jnp.log(r_sum) - r_hit
    matches = (reference_order[:, None] == jnp.arange(seq_count, dtype=jnp.int32)[None, :]).astype(
        jnp.float32
    )
    loss_reference = jnp.sum(
        matches[:, :, None] * loss_rows.reshape(seq_count, LENGTH)[:, None, :], axis=0
    ).reshape(tokens)
    first_row = lax.axis_index("dp") * rows_dp
    mine_target = lax.dynamic_slice_in_dim(loss_target, first_row, rows_dp, 0)
    mine_reference = lax.dynamic_slice_in_dim(loss_reference, first_row, rows_dp, 0)
    reducible = jnp.mean((mine_target - mine_reference).reshape(rows_dp // LENGTH, LENGTH), axis=1)
    return (mine_target, mine_reference, reducible)


def solution(mesh):
    placed = (
        P("dp", "mp"),
        P(),
        P(None, ("dp", "mp")),
        P(("dp", "mp"), None),
        P(),
        P(None, ("dp", "mp")),
        P("dp"),
        P(),
    )
    return jax.shard_map(
        shards, mesh=mesh, in_specs=placed, out_specs=(P("dp"), P("dp"), P("dp")), check_vma=False
    )
```

profile of v0, /device:TPU:0, one launch (start us, length us, event | category | flops | bytes accessed | tf_op | source)
XLA Modules:
  0.0 299.8 jit_solution(6555905454492770305)
XLA Ops:
  7.2 0.0 all-gather.5.cloned.1.call-start
  7.2 0.7 all-gather.5.cloned.1.call-update
  7.9 0.0 all-gather.9.cloned.1.call-start
  7.9 1.0 fusion.9
  9.0 1.7 fusion.11
  10.7 0.0 all-gather.9.cloned.1.call-update
  10.7 0.0 all-gather.7.cloned.1.call-start
  10.7 29.6 %all-gather.5.cloned.1.call-done = bf16[128,4096]{1,0:T(8,128)(2,1)} async-done(((bf16[128,1024]{1,0:T(8,128)(2,1)}), bf16[128,4096]{1,0:T(8,128)(2,1)}) %all-gather.5.cloned.1.call-update) | async-done | bytes 1048592 | tf_op jit(solution)/shard_map/all_gather | solution.py:41
  40.3 1.5 fusion.6
  41.8 2.6 fusion.8
  44.4 0.0 all-gather.7.cloned.1.call-update
  44.5 8.8 %all-gather = s32[8,1,128]{2,1,0:T(1,128)S(1)} all-gather(s32[1,1,128]{2,1,0:T(1,128)} %bitcast.56), channel_id=1, replica_groups=mesh['dp'=8,'mp'=4] {'dp'}, dimensions={0}, use_global_device_ids=true | all-gather | bytes 4608 | tf_op jit(solution)/shard_map/all_gather | solution.py:46
  53.3 0.7 compare_select_fusion
  54.0 0.6 gather_fusion
  54.5 0.7 compare_and_fusion
  55.2 0.1 broadcast_in_dim.48
  55.3 0.1 broadcast_bitcast_fusion
  55.4 1.3 fusion.12
  56.7 47.6 %all-gather.9.cloned.1.call-done = bf16[1024,2048]{1,0:T(8,128)(2,1)} async-done(((bf16[32,2048]{1,0:T(8,128)(2,1)}), bf16[1024,2048]{1,0:T(8,128)(2,1)}) %all-gather.9.cloned.1.call-update) | async-done | bytes 4194320 | tf_op jit(solution)/shard_map/all_gather | solution.py:56
  104.3 41.7 %while.15 = (s32[]{:T(128)}, f32[2,512]{1,0:T(2,128)S(1)}, f32[2,512]{1,0:T(2,128)S(1)}, f32[2,512]{1,0:T(2,128)S(1)}, bf16[2,512,2048]{2,1,0:T(8,128)(2,1)}, /*...) while((s32[]{:T(128)}, f32[2,512]{1,0:T(2,128)S(1)}, ...), condition=%wide.region_12.13_spmd.clone, body=%wide.region_8.12_spmd.clone.sunk | while | flops 8417700352 | bytes 34989508 | solution.py:66
  104.3 14.8 %fusion.21 = (f32[512]{0:T(512)S(1)}, f32[512,4008]{0,1:T(8,128)}) fusion(bf16[2048,4008]{0,1:T(8,128)(2,1)} %get-tuple-element.186, bf16[2,512,2048]{2,1,0:T(8,128)(2,1)} %get-tuple-element.185, s32[]{:T(128)S(6)} %copy.24), kind=kOutput, calls=%fused_computation.38.clone.1 | convolution fusion | flops 8407436800 | bytes 26724356 | tf_op jit(solution)/shard_map/while/body/eval_jaxpr/dot_general | solution.py:63
  119.2 5.1 %select_reduce_fusion.3 = (f32[512]{0:T(512)S(1)}, f32[512]{0:T(512)S(1)}) fusion(f32[512,4008]{0,1:T(8,128)} %get-tuple-element.158, s32[512]{0:T(512)S(1)} %bitcast.47, s32[4008]{0:T(1024)S(1)} %iota_add_fusion.3, f32[512]{0:T(512)S(1)} %get-tuple-element.157), kind=kLoop, calls=%fused_computation.2.clone.1 | loop fusion | flops 10259456 | bytes 8232608 | tf_op jit(solution)/shard_map/while/body/eval_jaxpr/reduce_sum | solution.py:20
  124.4 16.3 %fusion.21 = (f32[512]{0:T(512)S(1)}, f32[512,4008]{0,1:T(8,128)}) fusion(bf16[2048,4008]{0,1:T(8,128)(2,1)} %get-tuple-element.186, bf16[2,512,2048]{2,1,0:T(8,128)(2,1)} %get-tuple-element.185, s32[]{:T(128)S(6)} %copy.24), kind=kOutput, calls=%fused_computation.38.clone.1 | convolution fusion | flops 8407436800 | bytes 26724356 | tf_op jit(solution)/shard_map/while/body/eval_jaxpr/dot_general | solution.py:63
  140.7 5.3 %select_reduce_fusion.3 = (f32[512]{0:T(512)S(1)}, f32[512]{0:T(512)S(1)}) fusion(f32[512,4008]{0,1:T(8,128)} %get-tuple-element.158, s32[512]{0:T(512)S(1)} %bitcast.47, s32[4008]{0:T(1024)S(1)} %iota_add_fusion.3, f32[512]{0:T(512)S(1)} %get-tuple-element.157), kind=kLoop, calls=%fused_computation.2.clone.1 | loop fusion | flops 10259456 | bytes 8232608 | tf_op jit(solution)/shard_map/while/body/eval_jaxpr/reduce_sum | solution.py:20
  146.1 13.2 %all-gather.7.cloned.1.call-done = bf16[1024,4096]{1,0:T(8,128)(2,1)} async-done(((bf16[128,4096]{1,0:T(8,128)(2,1)}), bf16[1024,4096]{1,0:T(8,128)(2,1)}) %all-gather.7.cloned.1.call-update) | async-done | bytes 8388624 | tf_op jit(solution)/shard_map/all_gather | solution.py:45
  159.3 42.1 %fusion.14 = (f32[1024]{0:T(1024)S(1)}, f32[1024,4008]{0,1:T(8,128)}) fusion(bf16[1024,4096]{1,0:T(8,128)(2,1)} %all-gather.7.cloned.1.call-done, bf16[4096,4008]{0,1:T(8,128)(2,1)} %param.12), kind=kOutput, calls=%fused_computation.39 | convolution fusion | flops 33625645056 | bytes 57643008 | tf_op jit(solution)/shard_map/dot_general | solution.py:47
  201.4 39.5 %all-reduce.1 = (f32[1024]{0:T(1024)S(1)}, f32[1024]{0:T(1024)S(1)}) all-reduce(f32[1024]{0:T(1024)S(1)} %get-tuple-element.100, f32[1024]{0:T(1024)S(1)} %bitcast.48), channel_id=1, replica_groups=mesh['dp'=8,'mp'=4] {'dp','mp'}, use_global_device_ids=true, to_apply=%region_2.0 | all-reduce | flops 2048 | bytes 16384 | tf_op jit(solution)/shard_map/pmax | solution.py:73
  240.9 0.0 copy-start
  240.9 8.0 %exponential_reduce_fusion.1 = (f32[1024]{0:T(1024)S(1)}, f32[1024]{0:T(1024)S(1)}) fusion(f32[1024,4008]{0,1:T(8,128)} %get-tuple-element.101, f32[1024]{0:T(1024)S(1)} %get-tuple-element.100, s32[1024]{0:T(1024)S(1)} %bitcast.43, s32[4008]{0:T(1024)S(1)} %iota_add_fusion.1), kind=kLoop, calls=%fused_computation.11 | loop fusion | flops 20518912 | bytes 16449184 | tf_op jit(solution)/shard_map/reduce_sum | solution.py:19
  248.9 41.2 %all-reduce = (f32[1024]{0:T(1024)S(1)}, f32[1024]{0:T(1024)S(1)}, f32[1024]{0:T(1024)S(1)}, f32[1024]{0:T(1024)S(1)}) all-reduce(f32[1024]{0:T(1024)S(1)} %get-tuple-element.72, f32[1024]{0:T(1024)S(1)} %get-tuple-element.103, f32[1024]{0:T(1024)S(1)} %bitcast.50, ...), channel_id=1, replica_groups=mesh['dp'=8,'mp'=4] {'dp','mp'}, use_global_device_ids=true, to_apply=%region_6.7 | all-reduce | flops 4096 | bytes 32768 | tf_op jit(solution)/shard_map/psum | solution.py:74
  290.2 0.0 copy-done
  290.2 0.1 multiply_reduce_fusion
  290.3 1.2 subtract_reduce_fusion
  (25 shorter events, 0.3 us)
Async XLA Ops:
  7.2 33.1 %all-gather.5.cloned.1.call-start = ((), (), s32[]{:S(2)}) async-start(), calls=%async_computation | async-start | bytes 1310720 | tf_op jit(solution)/shard_map/all_gather | solution.py:41
  7.9 96.4 %all-gather.9.cloned.1.call-start = ((), (), s32[]{:S(2)}) async-start(), calls=%async_computation.2 | async-start | bytes 4325376 | tf_op jit(solution)/shard_map/all_gather | solution.py:56
  10.7 148.6 %all-gather.7.cloned.1.call-start = ((), (), s32[]{:S(2)}) async-start(), calls=%async_computation.1 | async-start | bytes 9437184 | tf_op jit(solution)/shard_map/all_gather | solution.py:45
  240.9 49.3 %copy-start = (f32[8,8]{1,0:T(8,128)S(1)}, f32[8,8]{1,0:T(8,128)}, u32[]{:S(2)}) copy-start(f32[8,8]{1,0:T(8,128)} %fusion.12) | copy-start | bytes 772
Sparse Core Ops, SparseCore 0:
  9.5 30.6 all-gather.4
  43.3 60.9 all-gather.8
  106.2 53.0 all-gather.6
where the time goes:
time: 300 us
  waiting for transfers between devices  91.1 us (30%)
  blocking collectives  89.6 us (30%)
  matrix products  73.2 us (24%)
  other arithmetic  29.1 us (10%)
  between operations  15.6 us (5%)
    all_gather x1, waiting for transfers between devices, shards(): ref_rows = lax.all_gather(ref_normed, ('dp', 'mp'), axis=0, tiled=True)  47.6 us
    dot_general x1, matrix products, shards(): logits = jnp.dot(rows_x, target_head, preferred_element_type=jnp.float32)  42.1 us
    psum x1, blocking collectives, shards(): lax.psum((t_total * jnp.exp(t_peak - t_max), t_pick, r_total * jnp.exp(r_...  41.2 us
    pmax x1, blocking collectives, shards(): t_max, r_max = lax.pmax((t_peak, r_peak), ('dp', 'mp'))  39.5 us
    dot_general x2, matrix products, ref_block(): logits = jnp.dot(rows_x, reference_head, preferred_element_type=jnp.float32)  31.1 us
    all_gather x1, waiting for transfers between devices, shards(): gathered = lax.all_gather(target_states, 'mp', axis=1, tiled=True)  29.6 us
    all_gather x1, waiting for transfers between devices, shards(): rows_x = lax.all_gather(normed, 'dp', axis=0, tiled=True)  13.2 us
    reduce_sum x2, other arithmetic, block_stats(): jnp.sum(jnp.where(columns[None, :] == rows_id[:, None], logits, 0.0), axi...  10.3 us
  transfers between devices with their start and end apart: 3, of which 3 were waited for; matrix products, arithmetic and copies ran while one was open for 17% of the time, Pallas kernels for 0%

commit v1 on v0

--- a/solution.py
+++ b/solution.py
@@ -38,7 +38,12 @@
     tokens = rows_dp * data_ways
     empty_float = jnp.zeros((tokens,), jnp.float32)
     empty_ids = jnp.zeros((tokens,), jnp.int32)
-    gathered = lax.all_gather(target_states, "mp", axis=1, tiled=True)
+    ring = [target_states]
+    for hop in range(3):
+        ring.append(lax.ppermute(ring[-1], "mp", [(dev, (dev + 1) % 4) for dev in range(4)]))
+    gathered = jnp.roll(
+        jnp.concatenate(ring[::-1], axis=1), (lax.axis_index("mp") + 1) * ring[0].shape[1], axis=1
+    )
     normed = normalize(gathered, target_gain)
     carry = (empty_float, empty_float, empty_float, empty_ids)
     start = jnp.int32(0)

time: 300 us -> 275 us (0.917)
  waiting for transfers between devices: 91.1 us -> 65.7 us
  other arithmetic: 29.1 us -> 24.8 us
  starting transfers between devices: 0.12 us -> 3.19 us
    all_gather x1 -> x0, waiting for transfers between devices: 29.6 us -> none  [shards(): gathered = lax.all_gather(target_states, 'mp', axis=1, tiled=True)]
    ppermute x0 -> x3, waiting for transfers between devices: none -> 28.1 us  [shards(): lax.ppermute(ring[-1], 'mp', [(dev, (dev + 1) % 4) for dev in range(4)])]
    all_gather x1, waiting for transfers between devices: 47.6 us -> 24.4 us  [shards(): ref_rows = lax.all_gather(ref_normed, ('dp', 'mp'), axis=0, tiled=True)]
    ppermute x0 -> x3, starting transfers between devices: none -> 3.11 us  [shards(): lax.ppermute(ring[-1], 'mp', [(dev, (dev + 1) % 4) for dev in range(4)])]
  transfers between devices with their start and end apart: 3 -> 5, of which waited for: 3 -> 5; matrix products, arithmetic and copies ran while one was open for 17% -> 17% of each run, Pallas kernels for 0% -> 0%
where the time goes in v1:
time: 275 us; the launch traced here: 274 us
  blocking collectives  89.2 us (32%)
  matrix products  73.2 us (27%)
  waiting for transfers between devices  65.7 us (24%)
  other arithmetic  24.8 us (9%)
  between operations  16 us (6%)
  starting transfers between devices  3.19 us (1%)
    dot_general x1, matrix products, shards(): logits = jnp.dot(rows_x, target_head, preferred_element_type=jnp.float32)  42.1 us
    psum x1, blocking collectives, shards(): lax.psum((t_total * jnp.exp(t_peak - t_max), t_pick, r_total * jnp.exp(r_...  41.3 us
    pmax x1, blocking collectives, shards(): t_max, r_max = lax.pmax((t_peak, r_peak), ('dp', 'mp'))  39.5 us
    dot_general x2, matrix products, ref_block(): logits = jnp.dot(rows_x, reference_head, preferred_element_type=jnp.float32)  31.1 us
    ppermute x3, waiting for transfers between devices, shards(): lax.ppermute(ring[-1], 'mp', [(dev, (dev + 1) % 4) for dev in range(4)])  28.1 us
    all_gather x1, waiting for transfers between devices, shards(): ref_rows = lax.all_gather(ref_normed, ('dp', 'mp'), axis=0, tiled=True)  24.4 us
    all_gather x1, waiting for transfers between devices, shards(): rows_x = lax.all_gather(normed, 'dp', axis=0, tiled=True)  13.2 us
    reduce_sum x2, other arithmetic, block_stats(): jnp.sum(jnp.where(columns[None, :] == rows_id[:, None], logits, 0.0), axi...  10.3 us
  transfers between devices with their start and end apart: 5, of which 5 were waited for; matrix products, arithmetic and copies ran while one was open for 17% of the time, Pallas kernels for 0%

profile of v1, /device:TPU:0, one launch (start us, length us, event | category | flops | bytes accessed | tf_op | source)
XLA Modules:
  0.0 274.4 jit_solution(16019566338811771452)
XLA Ops:
  7.2 0.0 copy-start
  7.2 0.0 copy-start.1
  7.2 0.0 all-gather.6.cloned.1.call-start
  7.2 1.1 fusion.9
  8.3 1.7 fusion.11
  10.0 0.0 all-gather.6.cloned.1.call-update
  10.0 0.0 all-gather.4.cloned.1.call-start
  10.0 3.1 %collective-permute-start = (bf16[128,1024]{1,0:T(8,128)(2,1)}, bf16[128,1024]{1,0:T(8,128)(2,1)S(1)}, u32[]{:S(2)}, u32[]{:S(2)}) collective-permute-start(bf16[128,1024]{1,0:T(8,128)(2,1)} %param.10), channel_id=1, source_target_pairs={{0,1},{1,2},{2,3},{3,0},{4,5},{5,6},{6,7},{7,4},{8,9},{9,10},{10,1... | collective-permute-start | bytes 786440 | tf_op jit(solution)/shard_map/ppermute | solution.py:43
  13.2 8.5 %collective-permute-done = bf16[128,1024]{1,0:T(8,128)(2,1)S(1)} collective-permute-done((bf16[128,1024]{1,0:T(8,128)(2,1)}, bf16[128,1024]{1,0:T(8,128)(2,1)S(1)}, u32[]{:S(2)}, u32[]{:S(2)}) %collective-permute-start) | collective-permute-done | bytes 262176 | tf_op jit(solution)/shard_map/ppermute | solution.py:43
  21.7 0.0 collective-permute-start.1
  21.7 11.4 %collective-permute-done.1 = bf16[128,1024]{1,0:T(8,128)(2,1)S(1)} collective-permute-done((bf16[128,1024]{1,0:T(8,128)(2,1)S(1)}, bf16[128,1024]{1,0:T(8,128)(2,1)S(1)}, u32[]{:S(2)}, u32[]{:S(2)}) %collective-permute-start.1) | collective-permute-done | bytes 262176 | tf_op jit(solution)/shard_map/ppermute | solution.py:43
  33.1 0.0 collective-permute-start.2
  33.1 0.0 copy-start.3
  33.1 0.0 copy-start.4
  33.1 8.2 %collective-permute-done.2 = bf16[128,1024]{1,0:T(8,128)(2,1)S(1)} collective-permute-done((bf16[128,1024]{1,0:T(8,128)(2,1)S(1)}, bf16[128,1024]{1,0:T(8,128)(2,1)S(1)}, u32[]{:S(2)}, u32[]{:S(2)}) %collective-permute-start.2) | collective-permute-done | bytes 262176 | tf_op jit(solution)/shard_map/ppermute | solution.py:43
  41.4 1.0 constant_dynamic-update-slice_fusion.4
  42.5 0.0 copy-done
  42.5 0.3 fusion.6
  42.8 0.0 copy-done.1
  42.8 1.4 fusion.8
  44.2 0.0 all-gather.4.cloned.1.call-update
  44.2 0.0 copy-done.3
  44.3 8.4 %all-gather = s32[8,1,128]{2,1,0:T(1,128)S(1)} all-gather(s32[1,1,128]{2,1,0:T(1,128)S(1)} %bitcast.56), channel_id=1, replica_groups=mesh['dp'=8,'mp'=4] {'dp'}, dimensions={0}, use_global_device_ids=true | all-gather | bytes 4608 | tf_op jit(solution)/shard_map/all_gather | solution.py:51
  52.7 0.0 copy-done.4
  52.7 0.6 gather_fusion
  53.3 0.1 broadcast_in_dim.48
  53.4 0.1 broadcast_bitcast_fusion
  53.4 0.7 fusion.12
  54.1 24.4 %all-gather.6.cloned.1.call-done = bf16[1024,2048]{1,0:T(8,128)(2,1)} async-done(((bf16[32,2048]{1,0:T(8,128)(2,1)}), bf16[1024,2048]{1,0:T(8,128)(2,1)}) %all-gather.6.cloned.1.call-update) | async-done | bytes 4194320 | tf_op jit(solution)/shard_map/all_gather | solution.py:61
  78.5 41.7 %while.15 = (s32[]{:T(128)}, f32[2,512]{1,0:T(2,128)S(1)}, f32[2,512]{1,0:T(2,128)S(1)}, f32[2,512]{1,0:T(2,128)S(1)}, bf16[2,512,2048]{2,1,0:T(8,128)(2,1)}, /*...) while((s32[]{:T(128)}, f32[2,512]{1,0:T(2,128)S(1)}, ...), condition=%wide.region_12.13_spmd.clone, body=%wide.region_8.12_spmd.clone.sunk | while | flops 8417700352 | bytes 34989508 | solution.py:71
  78.5 14.8 %fusion.21 = (f32[512]{0:T(512)S(1)}, f32[512,4008]{0,1:T(8,128)}) fusion(bf16[2048,4008]{0,1:T(8,128)(2,1)} %get-tuple-element.186, bf16[2,512,2048]{2,1,0:T(8,128)(2,1)} %get-tuple-element.185, s32[]{:T(128)S(6)} %copy.31), kind=kOutput, calls=%fused_computation.46.clone.1 | convolution fusion | flops 8407436800 | bytes 26724356 | tf_op jit(solution)/shard_map/while/body/eval_jaxpr/dot_general | solution.py:68
  93.4 5.1 %select_reduce_fusion.3 = (f32[512]{0:T(512)S(1)}, f32[512]{0:T(512)S(1)}) fusion(f32[512,4008]{0,1:T(8,128)} %get-tuple-element.158, s32[512]{0:T(512)S(1)} %bitcast.47, s32[4008]{0:T(1024)S(1)} %iota_add_fusion.3, f32[512]{0:T(512)S(1)} %get-tuple-element.157), kind=kLoop, calls=%fused_computation.2.clone.1 | loop fusion | flops 10259456 | bytes 8232608 | tf_op jit(solution)/shard_map/while/body/eval_jaxpr/reduce_sum | solution.py:20
  98.6 16.3 %fusion.21 = (f32[512]{0:T(512)S(1)}, f32[512,4008]{0,1:T(8,128)}) fusion(bf16[2048,4008]{0,1:T(8,128)(2,1)} %get-tuple-element.186, bf16[2,512,2048]{2,1,0:T(8,128)(2,1)} %get-tuple-element.185, s32[]{:T(128)S(6)} %copy.31), kind=kOutput, calls=%fused_computation.46.clone.1 | convolution fusion | flops 8407436800 | bytes 26724356 | tf_op jit(solution)/shard_map/while/body/eval_jaxpr/dot_general | solution.py:68
  114.9 5.3 %select_reduce_fusion.3 = (f32[512]{0:T(512)S(1)}, f32[512]{0:T(512)S(1)}) fusion(f32[512,4008]{0,1:T(8,128)} %get-tuple-element.158, s32[512]{0:T(512)S(1)} %bitcast.47, s32[4008]{0:T(1024)S(1)} %iota_add_fusion.3, f32[512]{0:T(512)S(1)} %get-tuple-element.157), kind=kLoop, calls=%fused_computation.2.clone.1 | loop fusion | flops 10259456 | bytes 8232608 | tf_op jit(solution)/shard_map/while/body/eval_jaxpr/reduce_sum | solution.py:20
  120.3 13.2 %all-gather.4.cloned.1.call-done = bf16[1024,4096]{1,0:T(8,128)(2,1)} async-done(((bf16[128,4096]{1,0:T(8,128)(2,1)}), bf16[1024,4096]{1,0:T(8,128)(2,1)}) %all-gather.4.cloned.1.call-update) | async-done | bytes 8388624 | tf_op jit(solution)/shard_map/all_gather | solution.py:50
  133.5 42.1 %fusion.14 = (f32[1024]{0:T(1024)S(1)}, f32[1024,4008]{0,1:T(8,128)}) fusion(bf16[1024,4096]{1,0:T(8,128)(2,1)} %all-gather.4.cloned.1.call-done, bf16[4096,4008]{0,1:T(8,128)(2,1)} %param.12), kind=kOutput, calls=%fused_computation.47 | convolution fusion | flops 33625645056 | bytes 57643008 | tf_op jit(solution)/shard_map/dot_general | solution.py:52
  175.6 39.5 %all-reduce.1 = (f32[1024]{0:T(1024)S(1)}, f32[1024]{0:T(1024)S(1)}) all-reduce(f32[1024]{0:T(1024)S(1)} %get-tuple-element.100, f32[1024]{0:T(1024)S(1)} %bitcast.48), channel_id=1, replica_groups=mesh['dp'=8,'mp'=4] {'dp','mp'}, use_global_device_ids=true, to_apply=%region_2.3 | all-reduce | flops 2048 | bytes 16384 | tf_op jit(solution)/shard_map/pmax | solution.py:78
  215.1 0.0 copy-start.2
  215.1 8.0 %exponential_reduce_fusion.1 = (f32[1024]{0:T(1024)S(1)}, f32[1024]{0:T(1024)S(1)}) fusion(f32[1024,4008]{0,1:T(8,128)} %get-tuple-element.101, f32[1024]{0:T(1024)S(1)} %get-tuple-element.100, s32[1024]{0:T(1024)S(1)} %bitcast.43, s32[4008]{0:T(1024)S(1)} %iota_add_fusion.1), kind=kLoop, calls=%fused_computation.11 | loop fusion | flops 20518912 | bytes 16449184 | tf_op jit(solution)/shard_map/reduce_sum | solution.py:19
  223.2 41.3 %all-reduce = (f32[1024]{0:T(1024)S(1)}, f32[1024]{0:T(1024)S(1)}, f32[1024]{0:T(1024)S(1)}, f32[1024]{0:T(1024)S(1)}) all-reduce(f32[1024]{0:T(1024)S(1)} %get-tuple-element.72, f32[1024]{0:T(1024)S(1)} %get-tuple-element.103, f32[1024]{0:T(1024)S(1)} %bitcast.50, ...), channel_id=1, replica_groups=mesh['dp'=8,'mp'=4] {'dp','mp'}, use_global_device_ids=true, to_apply=%region_6.7 | all-reduce | flops 4096 | bytes 32768 | tf_op jit(solution)/shard_map/psum | solution.py:79
  264.4 0.0 copy-done.2
  264.5 0.1 multiply_reduce_fusion
  264.5 1.2 subtract_reduce_fusion
  (34 shorter events, 0.5 us)
Async XLA Ops:
  7.2 35.3 %copy-start = (bf16[128,1024]{1,0:T(8,128)(2,1)S(1)}, bf16[128,1024]{1,0:T(8,128)(2,1)}, u32[]{:S(2)}) copy-start(bf16[128,1024]{1,0:T(8,128)(2,1)} %param.10) | copy-start | bytes 786436
  7.2 35.6 %copy-start.1 = (f32[4096]{0:T(1024)S(1)}, f32[4096]{0:T(1024)}, u32[]{:S(2)}) copy-start(f32[4096]{0:T(1024)} %param.11) | copy-start | bytes 49156
  7.2 71.3 %all-gather.6.cloned.1.call-start = ((), (), s32[]{:S(2)}) async-start(), calls=%async_computation.1 | async-start | bytes 4325376 | tf_op jit(solution)/shard_map/all_gather | solution.py:61
  10.0 123.5 %all-gather.4.cloned.1.call-start = ((), (), s32[]{:S(2)}) async-start(), calls=%async_computation | async-start | bytes 9437184 | tf_op jit(solution)/shard_map/all_gather | solution.py:50
  10.0 11.6 %collective-permute-start = (bf16[128,1024]{1,0:T(8,128)(2,1)}, bf16[128,1024]{1,0:T(8,128)(2,1)S(1)}, u32[]{:S(2)}, u32[]{:S(2)}) collective-permute-start(bf16[128,1024]{1,0:T(8,128)(2,1)} %param.10), channel_id=1, source_target_pairs={{0,1},{1,2},{2,3},{3,0},{4,5},{5,6},{6,7},{7,4},{8,9},{9,10},{10,1... | collective-permute-start | bytes 786440 | tf_op jit(solution)/shard_map/ppermute | solution.py:43
  21.7 11.4 %collective-permute-start.1 = (bf16[128,1024]{1,0:T(8,128)(2,1)S(1)}, bf16[128,1024]{1,0:T(8,128)(2,1)S(1)}, u32[]{:S(2)}, u32[]{:S(2)}) collective-permute-start(bf16[128,1024]{1,0:T(8,128)(2,1)S(1)} %collective-permute-done), channel_id=1, source_target_pairs={{0,1},{1,2},{2,3},{3,0},{4,5},{5,6},{6,7},{7,4},{8,9},{9,10},{10,1... | collective-permute-start | bytes 786440 | tf_op jit(solution)/shard_map/ppermute | solution.py:43
  33.1 8.2 %collective-permute-start.2 = (bf16[128,1024]{1,0:T(8,128)(2,1)S(1)}, bf16[128,1024]{1,0:T(8,128)(2,1)S(1)}, u32[]{:S(2)}, u32[]{:S(2)}) collective-permute-start(bf16[128,1024]{1,0:T(8,128)(2,1)S(1)} %collective-permute-done.1), channel_id=1, source_target_pairs={{0,1},{1,2},{2,3},{3,0},{4,5},{5,6},{6,7},{7,4},{8,9},{9,10},{10,1... | collective-permute-start | bytes 786440 | tf_op jit(solution)/shard_map/ppermute | solution.py:43
  33.1 11.1 %copy-start.3 = (s32[128]{0:T(128)S(1)}, s32[128]{0:T(128)}, u32[]{:S(2)}) copy-start(s32[128]{0:T(128)} %param.16) | copy-start | bytes 1540
  33.1 19.6 %copy-start.4 = (s32[8]{0:T(128)S(1)}, s32[8]{0:T(128)}, u32[]{:S(2)}) copy-start(s32[8]{0:T(128)} %param.17) | copy-start | bytes 100
  215.1 49.3 %copy-start.2 = (f32[8,8]{1,0:T(8,128)S(1)}, f32[8,8]{1,0:T(8,128)}, u32[]{:S(2)}) copy-start(f32[8,8]{1,0:T(8,128)} %fusion.12) | copy-start | bytes 772
Sparse Core Ops, SparseCore 0:
  11.0 67.4 all-gather.5
  80.4 53.0 all-gather.3
